TPU v7x, 32 devices: a whole 2x2x4 slice. The times are simulated.
32 devices in a mesh: cells: 8 (over y, x, core), obs: 4 (over z).
Axes of the slice: x: 2, y: 2, z: 4, core: 2. Of those that a mesh axis runs over, the one named last changes fastest.
Arguments:
- histories: bfloat16 [64, 384], P('obs'), may hold values from -6 to 6
- amplitude: bfloat16 [64, 5, 8192], P('obs', None, 'cells'), may hold values from -0.75 to 0.75
- weights: bfloat16 [8192, 256], P('cells'), may hold values from -0.375 to 0.375
- retarded: int32 [64, 64], P('obs', 'cells'), may hold values from 0 to 128
- owner_block: int32 [8192], P('cells'), may hold values from 0 to 7, as said below
- owner_cell: int32 [8192], P('cells'), may hold values from 0 to 16383
- adjoint: float32 [5, 16, 64, 128], P(None, 'cells', 'obs'), may hold values from -6 to 6
- step_size: float32 [16, 64, 128], P('cells', 'obs'), may hold values from 0.1 to 0.6
- jacobian: float32 [8, 3, 5, 5], P('cells'), may hold values from -6 to 6
Outputs:
- adjoint_next: float32 [5, 16, 64, 128], P(None, 'cells', 'obs')
- panel_source: float32 [5, 8192], P(None, 'cells')
Inputs may be any that keep to these rules, and one draw needn't show every extreme that they name: `owner_block`: among each device's 1024 panels at most 512 name one owner block; one owner block, drawn from the seed, is named by exactly 512 panels of every device.
All inputs are finite; a program needn't handle non-finite values.
Results may differ from a plain program's by a relative error of at most 0.0003.
Values sent between devices are 32-bit elements; how exact they have to be, the bound alone decides.
A program may use at most 192 MiB of HBM per device.

v0:
```python
import jax
import jax.numpy as jnp
from jax import lax
from jax.sharding import PartitionSpec as P

SAMPLES = 256
SPAN = 128
COMP = 5
TILE = 128
smoothing = 0.25


def extended(cells, sides, width, closed):
    for axis, dim in sides:
        count = lax.axis_size(axis)
        ends = count if closed else count - 1
        head = lax.slice_in_dim(cells, 0, width, axis=dim)
        tail = lax.slice_in_dim(cells, cells.shape[dim] - width, cells.shape[dim], axis=dim)
        cells = jnp.concatenate(
            [
                lax.ppermute(tail, axis, [(i, (i + 1) % count) for i in range(ends)]),
                cells,
                lax.ppermute(head, axis, [((i + 1) % count, i) for i in range(ends)]),
            ],
            axis=dim,
        )
    return cells


def on_device(
    histories, amplitude, weights, retarded, owner_block, owner_cell, adjoint, step_size, jacobian
):
    tile_count = weights.shape[0] // TILE
    weights_tiled = weights.reshape(tile_count, TILE, SAMPLES)
    observers_local = histories.shape[0]
    history_len = histories.shape[1]
    shifted = jnp.broadcast_to(histories[:, None, :], (observers_local, tile_count, history_len))
    for bit_number in range(SPAN.bit_length()):
        amount = 1 << bit_number
        moved = jnp.concatenate(
            [
                shifted[..., amount:],
                jnp.zeros((observers_local, tile_count, amount), shifted.dtype),
            ],
            axis=2,
        )
        chosen = retarded >> bit_number & 1 == 1
        shifted = jnp.where(chosen[:, :, None], moved, shifted)
    window = shifted[..., :SAMPLES]
    projected = jnp.einsum(
        "tps,ots->otp", weights_tiled, window, preferred_element_type=jnp.float32
    )
    projected = projected.reshape(projected.shape[0], -1)
    partial_value = jnp.sum(amplitude.astype(jnp.float32) * projected[:, None, :], axis=0)
    panel_source = lax.psum(partial_value, "obs")
    my_block = lax.axis_index("cells")
    my_group = lax.axis_index("obs")
    azimuth_local = adjoint.shape[1]
    radial_local = adjoint.shape[2]
    axial_len = adjoint.shape[3]
    radial_all = radial_local * lax.axis_size("obs")
    block_cells = azimuth_local * radial_all * axial_len
    device_cells = azimuth_local * radial_local * axial_len
    target = (owner_block * block_cells + owner_cell).reshape(1, -1)
    empty_field = jnp.zeros((COMP, device_cells), jnp.float32)
    devices = lax.axis_size("cells")
    capacity = 4 * owner_block.shape[0] // devices
    one_hot = (owner_block[:, None] == jnp.arange(devices, dtype=jnp.int32)[None, :]).astype(
        jnp.int32
    )
    slot_rank = jnp.sum(jnp.cumsum(one_hot, axis=0) * one_hot, axis=1) - 1
    slot_of = owner_block * capacity + slot_rank
    outgoing = jnp.zeros((COMP, devices * capacity), jnp.float32).at[:, slot_of].set(panel_source)
    out_index = jnp.full((1, devices * capacity), -1, jnp.int32).at[0, slot_of].set(target[0])
    received, arrivals = (
        lax.all_to_all(outgoing, "cells", split_axis=1, concat_axis=1, tiled=True),
        lax.all_to_all(out_index, "cells", split_axis=1, concat_axis=1, tiled=True),
    )
    flat_index = arrivals[0]
    block_of = flat_index // block_cells
    within = flat_index % block_cells
    azimuth = within // (radial_all * axial_len)
    radius = within // axial_len % radial_all
    axial = within % axial_len
    is_mine = (block_of == my_block) & (radius // radial_local == my_group) & (flat_index >= 0)
    position = (azimuth * radial_local + radius - my_group * radial_local) * axial_len + axial
    landing = jnp.where(is_mine, position, device_cells)
    surface = empty_field.at[:, landing].add(received, mode="drop")
    widened = extended(adjoint, (("cells", 1),), 1, True)
    heightened = extended(adjoint, (("obs", 2),), 1, False)
    deepened = jnp.pad(adjoint, ((0, 0), (0, 0), (0, 0), (1, 1)))
    matrices = jacobian[0]
    neighbours = (
        (widened[:, 2:], widened[:, :-2]),
        (heightened[:, :, 2:], heightened[:, :, :-2]),
        (deepened[..., 2:], deepened[..., :-2]),
    )
    summed = jnp.zeros_like(adjoint)
    for direction in range(3):
        forward, backward = neighbours[direction]
        rotated = jnp.einsum(
            "kc,karz->carz",
            matrices[direction],
            forward - backward,
            precision=lax.Precision.HIGHEST,
        )
        summed = summed + (0.5 * rotated + smoothing * (forward - 2.0 * adjoint + backward))
    adjoint_next = adjoint + step_size[None] * summed + surface.reshape(adjoint.shape)
    return (adjoint_next, panel_source)


def solution(mesh):
    return jax.shard_map(
        on_device,
        mesh=mesh,
        in_specs=(
            P("obs", None),
            P("obs", None, "cells"),
            P("cells", None),
            P("obs", "cells"),
            P("cells"),
            P("cells"),
            P(None, "cells", "obs", None),
            P("cells", "obs", None),
            P("cells", None, None, None),
        ),
        out_specs=(P(None, "cells", "obs", None), P(None, "cells")),
        check_vma=False,
    )
```

profile of v0, /device:TPU:0, one launch (start us, length us, event | category | flops | bytes accessed | tf_op | source)
XLA Modules:
  0.0 93.0 jit_solution(10608358137834040790)
XLA Ops:
  0.6 0.8 fusion.22
  1.4 2.3 %reduce-window.6 = s32[8,8,128]{2,1,0:T(8,128)S(1)} reduce-window(s32[8,8,128]{2,1,0:T(8,128)S(1)} %fusion.22, s32[]{:T(128)} %constant.118.clone.1), window={size=1x1x128 pad=0_0x0_0x127_0}, to_apply=%region_0.1 | reduce-window | flops 1040384 | bytes 65540 | tf_op jit(solution)/shard_map/reduce-window
  3.6 0.3 slice_reduce_fusion
  3.9 0.2 reduce-window.9
  4.1 0.1 add_bitcast_fusion
  4.2 0.7 fusion.21
  4.9 0.7 multiply_add_fusion
  5.6 0.7 fusion.25
  6.3 0.7 and_reduce_fusion
  7.1 4.9 %scatter_custom_fusion.2 = s32[4096]{0:T(1024)} fusion(s32[1024]{0:T(1024)S(1)} %broadcast_select_fusion, s32[1024]{0:T(1024)S(1)} %get-tuple-element.25, s32[]{:T(128)} %constant.116.clone.1), kind=kCustom, calls=%fused_computation.79 | custom fusion | bytes 16388
  12.0 5.2 %all-to-all-start = ((s32[1,8,512]{2,0,1:T(1,128)}), s32[1,8,512]{2,0,1:T(1,128)S(1)}, u32[]{:S(2)}, u32[]{:S(2)}) async-start(s32[1,8,512]{2,0,1:T(1,128)} %bitcast.12), calls=%async_computation | async-start | bytes 32768 | tf_op jit(solution)/shard_map/all_to_all | solution.py:77
  17.2 0.9 %copy.91 = f32[5,2,16,128]{3,0,2,1:T(8,128)S(1)} copy(f32[5,2,16,128]{3,2,1,0:T(8,128)} %param.15) | data formatting | bytes 163840 | tf_op args[6]
  18.1 1.3 %collective-permute-start.2 = (f32[5,2,1,128]{3,0,2,1:T(8,128)S(1)}, f32[5,2,1,128]{3,0,2,1:T(8,128)}, u32[]{:S(2)}, u32[]{:S(2)}) collective-permute-start(f32[5,2,1,128]{3,0,2,1:T(8,128)S(1)} %get-tuple-element.13), channel_id=1, source_target_pairs={{1,0},{2,1},{3,2},{5,4},{6,5},{7,6},{9,8},{10,9},{11,10},{13,12},{... | collective-permute-start | bytes 15368 | tf_op jit(solution)/shard_map/ppermute | solution.py:23
  19.4 5.1 %collective-permute-start.3 = (f32[5,2,1,128]{3,0,2,1:T(8,128)S(1)}, f32[5,2,1,128]{3,0,2,1:T(8,128)}, u32[]{:S(2)}, u32[]{:S(2)}) collective-permute-start(f32[5,2,1,128]{3,0,2,1:T(8,128)S(1)} %get-tuple-element.12), channel_id=1, source_target_pairs={{0,1},{1,2},{2,3},{4,5},{5,6},{6,7},{8,9},{9,10},{10,11},{12,13},{... | collective-permute-start | bytes 15368 | tf_op jit(solution)/shard_map/ppermute | solution.py:21
  24.6 0.6 fusion.32
  25.2 2.1 %collective-permute-start = (f32[5,1,16,128]{3,0,2,1:T(8,128)}, f32[5,1,16,128]{3,0,2,1:T(8,128)S(1)}, u32[]{:S(2)}, u32[]{:S(2)}) collective-permute-start(f32[5,1,16,128]{3,0,2,1:T(8,128)} %get-tuple-element.11), channel_id=1, source_target_pairs={{4,0},{8,4},{12,8},{16,12},{20,16},{24,20},{28,24},{0,28},{5,1},{9... | collective-permute-start | bytes 122888 | tf_op jit(solution)/shard_map/ppermute | solution.py:23
  27.3 0.7 and_compare_fusion.7
  28.0 0.8 slice.95
  28.8 0.8 pad_select_fusion.6
  29.6 0.1 slice.109
  29.7 0.9 pad_select_fusion.5
  30.6 0.1 slice.110
  30.7 0.8 pad_select_fusion.4
  31.5 0.1 slice.111
  31.6 0.1 pad_select_fusion.3
  31.7 0.1 slice.112
  31.8 0.1 pad_select_fusion.2
  31.9 0.1 slice.113
  32.0 0.1 pad_select_fusion.1
  32.1 0.1 slice.114
  32.2 0.1 pad_select_fusion
  32.4 0.3 convolution_bitcast_fusion
  32.6 0.0 copy-done.5
  32.7 1.1 %fusion.10 = f32[5,2,16,128]{3,0,2,1:T(8,128)} fusion(f32[5,2,16,128]{3,0,2,1:T(8,128)S(1)} %copy.91, f32[1,1,5,5]{3,0,2,1:T(1,128)S(1)} %get-tuple-element.16), kind=kOutput, calls=%fused_computation.16 | convolution fusion | flops 1372160 | bytes 346624 | tf_op jit(solution)/shard_map/kc,karz->carz/dot_general | solution.py:101
  33.8 0.1 multiply_reduce_fusion
  33.8 17.3 %psum.7 = f32[5,1024]{1,0:T(8,128)S(1)} all-reduce(f32[5,1024]{1,0:T(8,128)S(1)} %multiply_reduce_fusion), channel_id=1, replica_groups=mesh['cells'=8,'obs'=4] {'obs'}, use_global_device_ids=true, to_apply=%region_5.6 | all-reduce | flops 5120 | bytes 40960 | tf_op jit(solution)/shard_map/psum | solution.py:55
  51.2 0.2 copy.93
  51.4 3.6 %scatter_custom_fusion = f32[5,4096]{0,1:T(8,128)S(1)} fusion(s32[1024]{0:T(1024)S(1)} %get-tuple-element.26, f32[1024,5]{1,0:T(8,128)S(1)} %copy.93, f32[]{:T(128)} %constant.115.clone.1), kind=kCustom, calls=%fused_computation.20 | custom fusion | bytes 81924 | tf_op jit(solution)/shard_map/scatter | solution.py:73
  55.0 1.3 %copy.94 = f32[5,8,512]{2,0,1:T(8,128)} copy(f32[5,8,512]{0,2,1:T(8,128)S(1)} %bitcast.73) | data formatting | bytes 163840 | tf_op jit(solution)/shard_map/all_to_all | solution.py:76
  56.3 1.1 %fusion.9 = f32[5,2,16,128]{3,0,2,1:T(8,128)S(1)} fusion(f32[5,2,1,128]{3,0,2,1:T(8,128)} %collective-permute-done.2, f32[5,2,16,128]{3,0,2,1:T(8,128)S(1)} %copy.91, f32[5,2,1,128]{3,0,2,1:T(8,128)} %collective-permute-done.3, f32[1,1,5,5]{3,0,2,1:T(1,128)S(1)} %get-tuple-element.15), kind=kOutput, calls=%fused_computation.15 | convolution fusion | flops 1454080 | bytes 174180 | tf_op jit(solution)/shard_map/kc,karz->carz/dot_general | solution.py:101
  57.4 3.4 %all-to-all-start.1 = ((f32[5,8,512]{2,0,1:T(8,128)}), f32[5,8,512]{2,0,1:T(8,128)S(1)}, u32[]{:S(2)}, u32[]{:S(2)}) async-start(f32[5,8,512]{2,0,1:T(8,128)} %copy.94), calls=%async_computation.1 | async-start | bytes 262144 | tf_op jit(solution)/shard_map/all_to_all | solution.py:76
  60.8 0.5 compare_select_fusion
  61.3 5.0 %all-to-all-done.1 = f32[5,8,512]{2,0,1:T(8,128)S(1)} async-done(((f32[5,8,512]{2,0,1:T(8,128)}), f32[5,8,512]{2,0,1:T(8,128)S(1)}, u32[]{:S(2)}, u32[]{:S(2)}) %all-to-all-start.1) | async-done | bytes 81952 | tf_op jit(solution)/shard_map/all_to_all | solution.py:76
  66.2 2.0 %copy.95 = f32[4096,5]{1,0:T(8,128)} copy(f32[4096,5]{0,1:T(8,128)S(1)} %bitcast.74) | data formatting | bytes 163840 | tf_op jit(solution)/shard_map/all_to_all | solution.py:76
  68.2 23.2 %scatter_custom_fusion.1 = f32[5,4096]{0,1:T(8,128)S(1)} fusion(s32[4096]{0:T(1024)S(1)} %bitcast.82, f32[4096,5]{1,0:T(8,128)} %copy.95, f32[]{:T(128)} %constant.115.clone.1), kind=kCustom, calls=%fused_computation.18 | custom fusion | flops 20480 | bytes 82432 | tf_op jit(solution)/shard_map/scatter-add | solution.py:88
  91.4 0.6 copy.97
  92.0 0.3 fusion.8
  92.4 0.7 copy.98
  (23 shorter events, 0.1 us)
Async XLA Ops:
  0.6 31.7 %copy-start = (bf16[1024,256]{1,0:T(8,128)(2,1)S(1)}, bf16[1024,256]{1,0:T(8,128)(2,1)}, u32[]{:S(2)}) copy-start(bf16[1024,256]{1,0:T(8,128)(2,1)} %param.11) | copy-start | bytes 1572868
  12.0 45.4 %all-to-all-start = ((s32[1,8,512]{2,0,1:T(1,128)}), s32[1,8,512]{2,0,1:T(1,128)S(1)}, u32[]{:S(2)}, u32[]{:S(2)}) async-start(s32[1,8,512]{2,0,1:T(1,128)} %bitcast.12), calls=%async_computation | async-start | bytes 32768 | tf_op jit(solution)/shard_map/all_to_all | solution.py:77
  18.1 38.1 %collective-permute-start.2 = (f32[5,2,1,128]{3,0,2,1:T(8,128)S(1)}, f32[5,2,1,128]{3,0,2,1:T(8,128)}, u32[]{:S(2)}, u32[]{:S(2)}) collective-permute-start(f32[5,2,1,128]{3,0,2,1:T(8,128)S(1)} %get-tuple-element.13), channel_id=1, source_target_pairs={{1,0},{2,1},{3,2},{5,4},{6,5},{7,6},{9,8},{10,9},{11,10},{13,12},{... | collective-permute-start | bytes 15368 | tf_op jit(solution)/shard_map/ppermute | solution.py:23
  19.4 36.9 %collective-permute-start.3 = (f32[5,2,1,128]{3,0,2,1:T(8,128)S(1)}, f32[5,2,1,128]{3,0,2,1:T(8,128)}, u32[]{:S(2)}, u32[]{:S(2)}) collective-permute-start(f32[5,2,1,128]{3,0,2,1:T(8,128)S(1)} %get-tuple-element.12), channel_id=1, source_target_pairs={{0,1},{1,2},{2,3},{4,5},{5,6},{6,7},{8,9},{9,10},{10,11},{12,13},{... | collective-permute-start | bytes 15368 | tf_op jit(solution)/shard_map/ppermute | solution.py:21
  25.2 66.8 %collective-permute-start = (f32[5,1,16,128]{3,0,2,1:T(8,128)}, f32[5,1,16,128]{3,0,2,1:T(8,128)S(1)}, u32[]{:S(2)}, u32[]{:S(2)}) collective-permute-start(f32[5,1,16,128]{3,0,2,1:T(8,128)} %get-tuple-element.11), channel_id=1, source_target_pairs={{4,0},{8,4},{12,8},{16,12},{20,16},{24,20},{28,24},{0,28},{5,1},{9... | collective-permute-start | bytes 122888 | tf_op jit(solution)/shard_map/ppermute | solution.py:23
  27.3 64.7 %collective-permute-start.1 = (f32[5,1,16,128]{3,0,2,1:T(8,128)S(1)}, f32[5,1,16,128]{3,0,2,1:T(8,128)S(1)}, u32[]{:S(2)}, u32[]{:S(2)}) collective-permute-start(f32[5,1,16,128]{3,0,2,1:T(8,128)S(1)} %get-tuple-element.10), channel_id=1, source_target_pairs={{0,4},{4,8},{8,12},{12,16},{16,20},{20,24},{24,28},{28,0},{1,5},{5... | collective-permute-start | bytes 122888 | tf_op jit(solution)/shard_map/ppermute | solution.py:21
  28.8 3.9 %copy-start.5 = (f32[1,3,5,5]{3,0,2,1:T(1,128)S(1)}, f32[1,3,5,5]{3,0,2,1:T(1,128)}, u32[]{:S(2)}) copy-start(f32[1,3,5,5]{3,0,2,1:T(1,128)} %param.17) | copy-start | bytes 904
  29.7 4.0 %copy-start.1 = (bf16[16,5,1024]{2,0,1:T(8,128)(2,1)S(1)}, bf16[16,5,1024]{2,0,1:T(8,128)(2,1)}, u32[]{:S(2)}) copy-start(bf16[16,5,1024]{2,0,1:T(8,128)(2,1)} %param.10) | copy-start | bytes 491524
  51.2 5.1 %copy-start.2 = (f32[5,1024]{1,0:T(8,128)}, f32[5,1024]{1,0:T(8,128)S(1)}, u32[]{:S(2)}) copy-start(f32[5,1024]{1,0:T(8,128)S(1)} %psum.7) | copy-start | bytes 61444
  57.4 8.8 %all-to-all-start.1 = ((f32[5,8,512]{2,0,1:T(8,128)}), f32[5,8,512]{2,0,1:T(8,128)S(1)}, u32[]{:S(2)}, u32[]{:S(2)}) async-start(f32[5,8,512]{2,0,1:T(8,128)} %copy.94), calls=%async_computation.1 | async-start | bytes 262144 | tf_op jit(solution)/shard_map/all_to_all | solution.py:76
  68.2 23.8 %copy-start.3 = (f32[5,2,16,128]{3,0,2,1:T(8,128)S(1)}, f32[5,2,16,128]{3,0,2,1:T(8,128)}, u32[]{:S(2)}) copy-start(f32[5,2,16,128]{3,0,2,1:T(8,128)} %fusion.10) | copy-start | bytes 245764
  68.2 23.8 %copy-start.4 = (f32[2,16,128]{2,1,0:T(8,128)S(1)}, f32[2,16,128]{2,1,0:T(8,128)}, u32[]{:S(2)}) copy-start(f32[2,16,128]{2,1,0:T(8,128)} %param.16) | copy-start | bytes 49156
where the time goes:
time: 94.1 us; the launch traced here: 93 us
  other arithmetic  33.4 us (35%)
  blocking collectives  17.3 us (18%)
  starting transfers between devices  17.1 us (18%)
  local copies, waits for them, and re-layouts  16.5 us (18%)
  waiting for transfers between devices  4.98 us (5%)
  matrix products  2.79 us (3%)
    scatter-add x1, other arithmetic, on_device(): surface = empty_field.at[:, landing].add(received, mode='drop')  23.2 us
    psum x1, blocking collectives, on_device(): panel_source = lax.psum(partial_value, 'obs')  17.3 us
    unnamed x15, local copies, waits for them, and re-layouts  6.53 us
    all_to_all x1, starting transfers between devices, on_device(): lax.all_to_all(out_index, 'cells', split_axis=1, concat_axis=1, tiled=True)  5.2 us
    ppermute x2, starting transfers between devices, extended(): lax.ppermute(tail, axis, [(i, (i + 1) % count) for i in range(ends)])  5.15 us
    all_to_all x1, waiting for transfers between devices, on_device(): lax.all_to_all(outgoing, 'cells', split_axis=1, concat_axis=1, tiled=True)  4.97 us
    scatter x1, local copies, waits for them, and re-layouts, on_device(): jnp.zeros((COMP, devices * capacity), jnp.float32).at[:, slot_of]  3.59 us
    all_to_all x1, starting transfers between devices, on_device(): lax.all_to_all(outgoing, 'cells', split_axis=1, concat_axis=1, tiled=True)  3.38 us
  transfers between devices with their start and end apart: 6, of which 1 were waited for; matrix products, arithmetic and copies ran while one was open for 43% of the time, Pallas kernels for 0%

commit v1 on v0

--- a/solution.py
+++ b/solution.py
@@ -52,7 +52,16 @@
     )
     projected = projected.reshape(projected.shape[0], -1)
     partial_value = jnp.sum(amplitude.astype(jnp.float32) * projected[:, None, :], axis=0)
-    panel_source = lax.psum(partial_value, "obs")
+    num_devices = lax.axis_size("obs")
+    panel_source = partial_value
+    for k in [j for j in (1, 2, 4, 8, 16) if j < num_devices]:
+        store = []
+        j0 = 0
+        while j0 < num_devices:
+            store.append((j0, j0 ^ k))
+            j0 += 1
+        raw_out = lax.ppermute(panel_source, "obs", perm=store)
+        panel_source = panel_source + raw_out
     my_block = lax.axis_index("cells")
     my_group = lax.axis_index("obs")
     azimuth_local = adjoint.shape[1]

time: 94.1 us -> 77.1 us (0.82)
  blocking collectives: 17.3 us -> 0 us
  starting transfers between devices: 17.1 us -> 20.8 us
  other arithmetic: 33.4 us -> 30 us
  waiting for transfers between devices: 4.98 us -> 6.24 us
    psum x1 -> x0, blocking collectives: 17.3 us -> none  [on_device(): panel_source = lax.psum(partial_value, 'obs')]
    ppermute x0 -> x2, starting transfers between devices: none -> 5.77 us  [on_device(): raw_out = lax.ppermute(panel_source, 'obs', perm=store)]
    all_to_all x1, starting transfers between devices: 5.2 us -> 3.72 us  [on_device(): lax.all_to_all(out_index, 'cells', split_axis=1, concat_axis=1, tiled=True)]
    unnamed x4, other arithmetic: 1.57 us -> 0.26 us
    ppermute x0 -> x2, waiting for transfers between devices: none -> 1.26 us  [on_device(): raw_out = lax.ppermute(panel_source, 'obs', perm=store)]
    unnamed x15 -> x27, local copies, waits for them, and re-layouts: 6.53 us -> 5.68 us
  transfers between devices with their start and end apart: 6 -> 8, of which waited for: 1 -> 2; matrix products, arithmetic and copies ran while one was open for 43% -> 55% of each run, Pallas kernels for 0% -> 0%
where the time goes in v1:
time: 77.1 us; the launch traced here: 76.4 us
  other arithmetic  30 us (39%)
  starting transfers between devices  20.8 us (27%)
  local copies, waits for them, and re-layouts  15.7 us (20%)
  waiting for transfers between devices  6.24 us (8%)
  matrix products  2.66 us (3%)
  between operations  1.01 us (1%)
    scatter-add x1, other arithmetic, on_device(): surface = empty_field.at[:, landing].add(received, mode='drop')  23.2 us
    ppermute x2, starting transfers between devices, on_device(): raw_out = lax.ppermute(panel_source, 'obs', perm=store)  5.77 us
    unnamed x27, local copies, waits for them, and re-layouts  5.68 us
    all_to_all x1, waiting for transfers between devices, on_device(): lax.all_to_all(outgoing, 'cells', split_axis=1, concat_axis=1, tiled=True)  4.97 us
    ppermute x2, starting transfers between devices, extended(): lax.ppermute(tail, axis, [(i, (i + 1) % count) for i in range(ends)])  4.55 us
    all_to_all x1, starting transfers between devices, on_device(): lax.all_to_all(out_index, 'cells', split_axis=1, concat_axis=1, tiled=True)  3.72 us
    scatter x1, local copies, waits for them, and re-layouts, on_device(): jnp.zeros((COMP, devices * capacity), jnp.float32).at[:, slot_of]  3.59 us
    all_to_all x1, starting transfers between devices, on_device(): lax.all_to_all(outgoing, 'cells', split_axis=1, concat_axis=1, tiled=True)  3.37 us
  transfers between devices with their start and end apart: 8, of which 2 were waited for; matrix products, arithmetic and copies ran while one was open for 55% of the time, Pallas kernels for 0%

profile of v1, /device:TPU:0, one launch (start us, length us, event | category | flops | bytes accessed | tf_op | source)
XLA Modules:
  0.0 76.4 jit_solution(1670030182117314516)
XLA Ops:
  0.6 0.0 copy-start
  0.6 0.8 and_compare_fusion.7
  1.4 0.8 %slice.95 = bf16[16,383]{1,0:T(8,128)(2,1)S(1)} slice(bf16[16,384]{1,0:T(8,128)(2,1)} %param.9), slice={[0:16], [1:384]} | slice | bytes 24512 | tf_op jit(solution)/shard_map/slice | solution.py:42
  2.2 0.8 %pad_select_fusion.6 = bf16[16,8,384]{2,0,1:T(8,128)(2,1)S(1)} fusion(bf16[16,8,383]{2,0,1:T(8,128)(2,1)S(1)} %broadcast_in_dim.94, pred[16,8]{0,1:T(8,128)(4,1)S(1)} %get-tuple-element.23, bf16[16,384]{1,0:T(8,128)(2,1)} %param.9), kind=kLoop, calls=%fused_computation.38 | loop fusion | flops 49152 | bytes 208768 | tf_op jit(solution)/shard_map/jit(_where)/select_n | solution.py:48
  3.1 0.1 slice.109
  3.2 0.8 %pad_select_fusion.5 = bf16[16,8,384]{2,0,1:T(8,128)(2,1)S(1)} fusion(bf16[16,8,382]{2,0,1:T(8,128)(2,1)S(1)} %slice.109, pred[16,8]{0,1:T(8,128)(4,1)S(1)} %get-tuple-element.24, bf16[16,384]{1,0:T(8,128)(2,1)} %param.9, bf16[16,8,383]{2,0,1:T(8,128)(2,1)S(1)} %broadcast_in_dim.94, pred[16,8]{0,1:T(8,128)(4,1)S(1)} %get-tuple-element.23), kind=kLoop, calls=%fused_computation.37 | loop fusion | flops 98304 | bytes 306688 | tf_op jit(solution)/shard_map/jit(_where)/select_n | solution.py:48
  4.0 0.1 slice.110
  4.1 0.8 %pad_select_fusion.4 = bf16[16,8,384]{2,0,1:T(8,128)(2,1)S(1)} fusion(bf16[16,8,380]{2,0,1:T(8,128)(2,1)S(1)} %slice.110, pred[16,8]{0,1:T(8,128)(4,1)S(1)} %get-tuple-element.18, bf16[16,384]{1,0:T(8,128)(2,1)} %param.9, bf16[16,8,383]{2,0,1:T(8,128)(2,1)S(1)} %broadcast_in_dim.94, pred[16,8]{0,1:T(8,128)(4,1)S(1)} %get-tuple-element.23, ...), kind=kLoop, calls=%fused_computation.36 | loop fusion | flops 147456 | bytes 404096 | tf_op jit(solution)/shard_map/jit(_where)/select_n | solution.py:48
  5.0 0.1 slice.111
  5.1 0.1 pad_select_fusion.3
  5.2 0.1 slice.112
  5.3 0.1 pad_select_fusion.2
  5.4 0.1 slice.113
  5.5 0.1 pad_select_fusion.1
  5.6 0.1 slice.114
  5.7 0.1 pad_select_fusion
  5.8 0.3 convolution_bitcast_fusion
  6.1 0.0 copy-done.1
  6.1 0.1 multiply_reduce_fusion
  6.2 3.1 %collective-permute-start.4 = (f32[5,1024]{1,0:T(8,128)S(1)}, f32[5,1024]{1,0:T(8,128)S(1)}, u32[]{:S(2)}, u32[]{:S(2)}) collective-permute-start(f32[5,1024]{1,0:T(8,128)S(1)} %multiply_reduce_fusion), channel_id=1, source_target_pairs={{0,1},{1,0},{2,3},{3,2},{4,5},{5,4},{6,7},{7,6},{8,9},{9,8},{10,11... | collective-permute-start | bytes 61448 | tf_op jit(solution)/shard_map/ppermute | solution.py:63
  9.3 2.3 %reduce-window.6 = s32[8,8,128]{2,1,0:T(8,128)S(1)} reduce-window(s32[8,8,128]{2,1,0:T(8,128)S(1)} %fusion.22, s32[]{:T(128)} %constant.118.clone.1), window={size=1x1x128 pad=0_0x0_0x127_0}, to_apply=%region_0.1 | reduce-window | flops 1040384 | bytes 65540 | tf_op jit(solution)/shard_map/reduce-window
  11.6 0.3 slice_reduce_fusion
  11.9 0.2 reduce-window.9
  12.1 0.1 add_bitcast_fusion
  12.2 0.1 fusion.25
  12.3 0.1 and_reduce_fusion
  12.4 4.9 %scatter_custom_fusion.2 = s32[4096]{0:T(1024)} fusion(s32[1024]{0:T(1024)S(1)} %broadcast_select_fusion, s32[1024]{0:T(1024)S(1)} %get-tuple-element.25, s32[]{:T(128)} %constant.116.clone.1), kind=kCustom, calls=%fused_computation.79 | custom fusion | bytes 16388
  17.3 3.7 %all-to-all-start = ((s32[1,8,512]{2,0,1:T(1,128)}), s32[1,8,512]{2,0,1:T(1,128)S(1)}, u32[]{:S(2)}, u32[]{:S(2)}) async-start(s32[1,8,512]{2,0,1:T(1,128)} %bitcast.12), calls=%async_computation | async-start | bytes 32768 | tf_op jit(solution)/shard_map/all_to_all | solution.py:86
  21.0 0.1 copy.91
  21.1 1.3 %collective-permute-start.2 = (f32[5,2,1,128]{3,0,2,1:T(8,128)S(1)}, f32[5,2,1,128]{3,0,2,1:T(8,128)S(1)}, u32[]{:S(2)}, u32[]{:S(2)}) collective-permute-start(f32[5,2,1,128]{3,0,2,1:T(8,128)S(1)} %get-tuple-element.13), channel_id=1, source_target_pairs={{1,0},{2,1},{3,2},{5,4},{6,5},{7,6},{9,8},{10,9},{11,10},{13,12},{... | collective-permute-start | bytes 15368 | tf_op jit(solution)/shard_map/ppermute | solution.py:23
  22.4 4.5 %collective-permute-start.3 = (f32[5,2,1,128]{3,0,2,1:T(8,128)S(1)}, f32[5,2,1,128]{3,0,2,1:T(8,128)S(1)}, u32[]{:S(2)}, u32[]{:S(2)}) collective-permute-start(f32[5,2,1,128]{3,0,2,1:T(8,128)S(1)} %get-tuple-element.12), channel_id=1, source_target_pairs={{0,1},{1,2},{2,3},{4,5},{5,6},{6,7},{8,9},{9,10},{10,11},{12,13},{... | collective-permute-start | bytes 15368 | tf_op jit(solution)/shard_map/ppermute | solution.py:21
  26.9 0.6 fusion.32
  27.6 2.1 %collective-permute-start = (f32[5,1,16,128]{3,0,2,1:T(8,128)}, f32[5,1,16,128]{3,0,2,1:T(8,128)S(1)}, u32[]{:S(2)}, u32[]{:S(2)}) collective-permute-start(f32[5,1,16,128]{3,0,2,1:T(8,128)} %get-tuple-element.11), channel_id=1, source_target_pairs={{4,0},{8,4},{12,8},{16,12},{20,16},{24,20},{28,24},{0,28},{5,1},{9... | collective-permute-start | bytes 122888 | tf_op jit(solution)/shard_map/ppermute | solution.py:23
  29.7 1.1 %fusion.10 = f32[5,2,16,128]{3,0,2,1:T(8,128)} fusion(f32[5,2,16,128]{3,0,2,1:T(8,128)S(1)} %copy.91, f32[1,1,5,5]{3,0,2,1:T(1,128)S(1)} %get-tuple-element.16), kind=kOutput, calls=%fused_computation.16 | convolution fusion | flops 1372160 | bytes 346624 | tf_op jit(solution)/shard_map/kc,karz->carz/dot_general | solution.py:110
  30.7 2.7 %collective-permute-start.5 = (f32[5,1024]{1,0:T(8,128)S(1)}, f32[5,1024]{1,0:T(8,128)S(1)}, u32[]{:S(2)}, u32[]{:S(2)}) collective-permute-start(f32[5,1024]{1,0:T(8,128)S(1)} %add.185), channel_id=1, source_target_pairs={{0,2},{1,3},{2,0},{3,1},{4,6},{5,7},{6,4},{7,5},{8,10},{9,11},{10,... | collective-permute-start | bytes 61448 | tf_op jit(solution)/shard_map/ppermute | solution.py:63
  33.4 1.0 %fusion.9 = f32[5,2,16,128]{3,0,2,1:T(8,128)} fusion(f32[5,2,1,128]{3,0,2,1:T(8,128)S(1)} %collective-permute-done.2, f32[5,2,16,128]{3,0,2,1:T(8,128)S(1)} %copy.91, f32[5,2,1,128]{3,0,2,1:T(8,128)S(1)} %collective-permute-done.3, f32[1,1,5,5]{3,0,2,1:T(1,128)S(1)} %get-tuple-element.15), kind=kOutput, calls=%fused_computation.15 | convolution fusion | flops 1454080 | bytes 174180 | tf_op jit(solution)/shard_map/kc,karz->carz/dot_general | solution.py:110
  34.4 1.3 %collective-permute-done.5 = f32[5,1024]{1,0:T(8,128)S(1)} collective-permute-done((f32[5,1024]{1,0:T(8,128)S(1)}, f32[5,1024]{1,0:T(8,128)S(1)}, u32[]{:S(2)}, u32[]{:S(2)}) %collective-permute-start.5) | collective-permute-done | bytes 20512 | tf_op jit(solution)/shard_map/ppermute | solution.py:63
  35.6 0.2 copy.93
  35.9 3.6 %scatter_custom_fusion = f32[5,4096]{0,1:T(8,128)S(1)} fusion(s32[1024]{0:T(1024)S(1)} %get-tuple-element.26, f32[1024,5]{1,0:T(8,128)S(1)} %copy.93, f32[]{:T(128)} %constant.115.clone.1), kind=kCustom, calls=%fused_computation.20 | custom fusion | bytes 81924 | tf_op jit(solution)/shard_map/scatter | solution.py:82
  39.5 1.3 %copy.94 = f32[5,8,512]{2,0,1:T(8,128)} copy(f32[5,8,512]{0,2,1:T(8,128)S(1)} %bitcast.73) | data formatting | bytes 163840 | tf_op jit(solution)/shard_map/all_to_all | solution.py:85
  40.7 3.4 %all-to-all-start.1 = ((f32[5,8,512]{2,0,1:T(8,128)}), f32[5,8,512]{2,0,1:T(8,128)S(1)}, u32[]{:S(2)}, u32[]{:S(2)}) async-start(f32[5,8,512]{2,0,1:T(8,128)} %copy.94), calls=%async_computation.1 | async-start | bytes 262144 | tf_op jit(solution)/shard_map/all_to_all | solution.py:85
  44.1 0.5 compare_select_fusion
  44.6 5.0 %all-to-all-done.1 = f32[5,8,512]{2,0,1:T(8,128)S(1)} async-done(((f32[5,8,512]{2,0,1:T(8,128)}), f32[5,8,512]{2,0,1:T(8,128)S(1)}, u32[]{:S(2)}, u32[]{:S(2)}) %all-to-all-start.1) | async-done | bytes 81952 | tf_op jit(solution)/shard_map/all_to_all | solution.py:85
  49.6 2.0 %copy.95 = f32[4096,5]{1,0:T(8,128)} copy(f32[4096,5]{0,1:T(8,128)S(1)} %bitcast.74) | data formatting | bytes 163840 | tf_op jit(solution)/shard_map/all_to_all | solution.py:85
  51.6 23.2 %scatter_custom_fusion.1 = f32[5,4096]{0,1:T(8,128)S(1)} fusion(s32[4096]{0:T(1024)S(1)} %bitcast.82, f32[4096,5]{1,0:T(8,128)} %copy.95, f32[]{:T(128)} %constant.115.clone.1), kind=kCustom, calls=%fused_computation.18 | custom fusion | flops 20480 | bytes 82432 | tf_op jit(solution)/shard_map/scatter-add | solution.py:97
  74.7 0.6 copy.97
  75.4 0.3 fusion.8
  75.7 0.7 copy.98
  (40 shorter events, 0.2 us)
Async XLA Ops:
  0.6 5.2 %copy-start = (bf16[1024,256]{1,0:T(8,128)(2,1)S(1)}, bf16[1024,256]{1,0:T(8,128)(2,1)}, u32[]{:S(2)}) copy-start(bf16[1024,256]{1,0:T(8,128)(2,1)} %param.11) | copy-start | bytes 1572868
  2.2 3.9 %copy-start.1 = (bf16[16,5,1024]{2,0,1:T(8,128)(2,1)S(1)}, bf16[16,5,1024]{2,0,1:T(8,128)(2,1)}, u32[]{:S(2)}) copy-start(bf16[16,5,1024]{2,0,1:T(8,128)(2,1)} %param.10) | copy-start | bytes 491524
  3.2 6.2 %copy-start.6 = (s32[1024]{0:T(1024)S(1)}, s32[1024]{0:T(1024)}, u32[]{:S(2)}) copy-start(s32[1024]{0:T(1024)} %param.13) | copy-start | bytes 12292
  4.0 8.2 %copy-start.9 = (s32[1024]{0:T(1024)S(1)}, s32[1024]{0:T(1024)}, u32[]{:S(2)}) copy-start(s32[1024]{0:T(1024)} %param.14) | copy-start | bytes 12292
  4.0 8.2 %copy-start.10 = (s32[2]{0:T(128)S(1)}, s32[2]{0:T(128)}, u32[]{:S(2)}) copy-start(s32[2]{0:T(128)} %constant.165) | copy-start | bytes 28
  4.0 8.3 %copy-start.11 = (s32[2]{0:T(128)S(1)}, s32[2]{0:T(128)}, u32[]{:S(2)}) copy-start(s32[2]{0:T(128)} %constant.168) | copy-start | bytes 28
  4.0 17.0 %copy-start.5 = (f32[5,2,16,128]{3,2,1,0:T(8,128)S(1)}, f32[5,2,16,128]{3,2,1,0:T(8,128)}, u32[]{:S(2)}) copy-start(f32[5,2,16,128]{3,2,1,0:T(8,128)} %param.15) | copy-start | bytes 245764
  5.0 24.7 %copy-start.8 = (f32[1,3,5,5]{3,0,2,1:T(1,128)S(1)}, f32[1,3,5,5]{3,0,2,1:T(1,128)}, u32[]{:S(2)}) copy-start(f32[1,3,5,5]{3,0,2,1:T(1,128)} %param.17) | copy-start | bytes 904
  6.2 24.5 %collective-permute-start.4 = (f32[5,1024]{1,0:T(8,128)S(1)}, f32[5,1024]{1,0:T(8,128)S(1)}, u32[]{:S(2)}, u32[]{:S(2)}) collective-permute-start(f32[5,1024]{1,0:T(8,128)S(1)} %multiply_reduce_fusion), channel_id=1, source_target_pairs={{0,1},{1,0},{2,3},{3,2},{4,5},{5,4},{6,7},{7,6},{8,9},{9,8},{10,11... | collective-permute-start | bytes 61448 | tf_op jit(solution)/shard_map/ppermute | solution.py:63
  17.3 23.5 %all-to-all-start = ((s32[1,8,512]{2,0,1:T(1,128)}), s32[1,8,512]{2,0,1:T(1,128)S(1)}, u32[]{:S(2)}, u32[]{:S(2)}) async-start(s32[1,8,512]{2,0,1:T(1,128)} %bitcast.12), calls=%async_computation | async-start | bytes 32768 | tf_op jit(solution)/shard_map/all_to_all | solution.py:86
  21.1 12.3 %collective-permute-start.2 = (f32[5,2,1,128]{3,0,2,1:T(8,128)S(1)}, f32[5,2,1,128]{3,0,2,1:T(8,128)S(1)}, u32[]{:S(2)}, u32[]{:S(2)}) collective-permute-start(f32[5,2,1,128]{3,0,2,1:T(8,128)S(1)} %get-tuple-element.13), channel_id=1, source_target_pairs={{1,0},{2,1},{3,2},{5,4},{6,5},{7,6},{9,8},{10,9},{11,10},{13,12},{... | collective-permute-start | bytes 15368 | tf_op jit(solution)/shard_map/ppermute | solution.py:23
  22.4 11.0 %collective-permute-start.3 = (f32[5,2,1,128]{3,0,2,1:T(8,128)S(1)}, f32[5,2,1,128]{3,0,2,1:T(8,128)S(1)}, u32[]{:S(2)}, u32[]{:S(2)}) collective-permute-start(f32[5,2,1,128]{3,0,2,1:T(8,128)S(1)} %get-tuple-element.12), channel_id=1, source_target_pairs={{0,1},{1,2},{2,3},{4,5},{5,6},{6,7},{8,9},{9,10},{10,11},{12,13},{... | collective-permute-start | bytes 15368 | tf_op jit(solution)/shard_map/ppermute | solution.py:21
  27.6 47.8 %collective-permute-start = (f32[5,1,16,128]{3,0,2,1:T(8,128)}, f32[5,1,16,128]{3,0,2,1:T(8,128)S(1)}, u32[]{:S(2)}, u32[]{:S(2)}) collective-permute-start(f32[5,1,16,128]{3,0,2,1:T(8,128)} %get-tuple-element.11), channel_id=1, source_target_pairs={{4,0},{8,4},{12,8},{16,12},{20,16},{24,20},{28,24},{0,28},{5,1},{9... | collective-permute-start | bytes 122888 | tf_op jit(solution)/shard_map/ppermute | solution.py:23
  29.6 45.7 %collective-permute-start.1 = (f32[5,1,16,128]{3,0,2,1:T(8,128)S(1)}, f32[5,1,16,128]{3,0,2,1:T(8,128)S(1)}, u32[]{:S(2)}, u32[]{:S(2)}) collective-permute-start(f32[5,1,16,128]{3,0,2,1:T(8,128)S(1)} %get-tuple-element.10), channel_id=1, source_target_pairs={{0,4},{4,8},{8,12},{12,16},{16,20},{20,24},{24,28},{28,0},{1,5},{5... | collective-permute-start | bytes 122888 | tf_op jit(solution)/shard_map/ppermute | solution.py:21
  30.7 4.9 %collective-permute-start.5 = (f32[5,1024]{1,0:T(8,128)S(1)}, f32[5,1024]{1,0:T(8,128)S(1)}, u32[]{:S(2)}, u32[]{:S(2)}) collective-permute-start(f32[5,1024]{1,0:T(8,128)S(1)} %add.185), channel_id=1, source_target_pairs={{0,2},{1,3},{2,0},{3,1},{4,6},{5,7},{6,4},{7,5},{8,10},{9,11},{10,... | collective-permute-start | bytes 61448 | tf_op jit(solution)/shard_map/ppermute | solution.py:63
  35.6 5.1 %copy-start.2 = (f32[5,1024]{1,0:T(8,128)}, f32[5,1024]{1,0:T(8,128)S(1)}, u32[]{:S(2)}) copy-start(f32[5,1024]{1,0:T(8,128)S(1)} %add.186) | copy-start | bytes 61444
  40.7 8.8 %all-to-all-start.1 = ((f32[5,8,512]{2,0,1:T(8,128)}), f32[5,8,512]{2,0,1:T(8,128)S(1)}, u32[]{:S(2)}, u32[]{:S(2)}) async-start(f32[5,8,512]{2,0,1:T(8,128)} %copy.94), calls=%async_computation.1 | async-start | bytes 262144 | tf_op jit(solution)/shard_map/all_to_all | solution.py:85
  51.5 23.8 %copy-start.3 = (f32[5,2,16,128]{3,0,2,1:T(8,128)S(1)}, f32[5,2,16,128]{3,0,2,1:T(8,128)}, u32[]{:S(2)}) copy-start(f32[5,2,16,128]{3,0,2,1:T(8,128)} %fusion.10) | copy-start | bytes 245764
  51.5 23.8 %copy-start.4 = (f32[5,2,16,128]{3,0,2,1:T(8,128)S(1)}, f32[5,2,16,128]{3,0,2,1:T(8,128)}, u32[]{:S(2)}) copy-start(f32[5,2,16,128]{3,0,2,1:T(8,128)} %fusion.9) | copy-start | bytes 245764
  51.5 23.8 %copy-start.7 = (f32[2,16,128]{2,1,0:T(8,128)S(1)}, f32[2,16,128]{2,1,0:T(8,128)}, u32[]{:S(2)}) copy-start(f32[2,16,128]{2,1,0:T(8,128)} %param.16) | copy-start | bytes 49156
